TPU v7x, 128 devices: a whole 4x4x4 slice. The times are simulated.
128 devices in a mesh: row: 8 (over z, core), col: 16 (over y, x).
Axes of the slice: x: 4, y: 4, z: 4, core: 2. Of those that a mesh axis runs over, the one named last changes fastest.
Arguments:
- emb: bfloat16 [524288, 512], P(('row', 'col')), may hold values from -6 to 6
- tiles: bfloat16 [2048, 4, 256, 256], P(('row', 'col')), may hold values from -0.375 to 0.375
- msg_src: int32 [2048, 4], P(('row', 'col')), may hold values from 0 to 15
- msg_dst: int32 [2048, 4], P(('row', 'col')), may hold values from 0 to 16, as said below
- msg_count: int32 [2048, 4], P(('row', 'col')), may hold values from 1 to 256
- weight: bfloat16 [512, 512], replicated, may hold values from -0.25 to 0.25
- docs: bfloat16 [512, 512], P('row'), may hold values from -0.059814453 to 0.099609375
- doc_labels: int32 [512, 8], replicated, may hold values from 0 to 524287
Outputs:
- hidden: bfloat16 [524288, 512], P(('row', 'col'))
- grad_docs: float32 [512, 512], P('row')
- grad_weight: float32 [512, 512], replicated
Inputs may be any that keep to these rules, and one draw needn't show every extreme that they name: For each sending device and each column of its row, the used slots (msg_dst below 16) come first and 16 marks an unused slot. In every row of devices some column receives all 4 slots used from every sender of that row.
All inputs are finite; a program needn't handle non-finite values.
Results may differ from a plain program's by a relative error of at most 0.0052.
Values may be sent and summed in bfloat16 or wider, within the bound.
No kernel may reach another device: no remote copies, remote signals or barrier semaphores. Data moves between devices by JAX's collectives and lax.ppermute only.
A program may use at most 192 MiB of HBM per device.

v0:
```python
import jax
import jax.numpy as jnp
from jax import lax
from jax.sharding import PartitionSpec as P


def per_device(emb, tiles, msg_src, msg_dst, msg_count, weight, docs, doc_labels):
    n_col = lax.axis_size("col")
    n_row = lax.axis_size("row")
    label_dev, width = emb.shape
    blk = tiles.shape[-1]
    cap = tiles.shape[1]
    blk_dev = label_dev // blk
    labels_total = float(label_dev * n_row * n_col)
    pos_count = doc_labels.shape[1]
    own_blocks = emb.reshape(blk_dev, blk, width)
    picked = own_blocks[msg_src]
    messages = jnp.einsum(
        "pqij,pqjd->pqid", tiles, picked, preferred_element_type=jnp.float32
    ).astype(jnp.bfloat16)
    received, dst_seen, cnt_seen = (
        lax.all_to_all(messages, "col", split_axis=0, concat_axis=0, tiled=True),
        lax.all_to_all(
            msg_dst.astype(jnp.bfloat16), "col", split_axis=0, concat_axis=0, tiled=True
        ),
        lax.all_to_all(
            msg_count.astype(jnp.bfloat16), "col", split_axis=0, concat_axis=0, tiled=True
        ),
    )
    slots_all = n_col * cap
    block_ids = jnp.arange(blk_dev, dtype=jnp.float32)
    hot = (dst_seen.astype(jnp.float32).reshape(1, slots_all) == block_ids[:, None]).astype(
        jnp.float32
    )
    weighted = hot * cnt_seen.astype(jnp.float32).reshape(1, slots_all)
    total = jnp.dot(
        weighted.astype(jnp.bfloat16),
        received.reshape(slots_all, blk * width),
        preferred_element_type=jnp.float32,
    ).reshape(blk_dev, blk, width)
    total = total + float(blk) * own_blocks.astype(jnp.float32)
    denom = float(blk) + jnp.sum(weighted, axis=1)
    agg = (total / denom[:, None, None]).astype(jnp.bfloat16).reshape(label_dev, width)
    pre = jnp.dot(agg, weight, preferred_element_type=jnp.float32)
    hidden = jax.nn.silu(pre).astype(jnp.bfloat16)
    device = lax.axis_index("row") * n_col + lax.axis_index("col")
    label_ids = device * label_dev + jnp.arange(label_dev, dtype=jnp.int32)
    piece = lax.all_gather(docs, "row", axis=0, tiled=True)
    scores = jnp.einsum("nd,ld->nl", piece, hidden, preferred_element_type=jnp.float32)
    positive = doc_labels[:, 0:1] == label_ids[None, :]
    for which in range(1, pos_count):
        positive = positive | (doc_labels[:, which : which + 1] == label_ids[None, :])
    prob = jax.nn.sigmoid(scores)
    dscore = jnp.where(positive, (prob - 1.0) / float(pos_count), prob / labels_total).astype(
        jnp.bfloat16
    )
    rows_grad = jnp.dot(dscore, hidden, preferred_element_type=jnp.float32)
    dhid = jnp.einsum("nl,nd->ld", dscore, piece, preferred_element_type=jnp.float32)
    doc_grad = rows_grad
    dhid, doc_grad = (dhid, doc_grad)
    sig = jax.nn.sigmoid(pre)
    dpre = (dhid * sig * (1.0 + pre * (1.0 - sig))).astype(jnp.bfloat16)
    weight_part = jnp.einsum("la,lb->ab", agg, dpre, preferred_element_type=jnp.float32)
    grad_weight = lax.psum(weight_part, ("row", "col"))
    row_share = lax.psum_scatter(doc_grad, "row", scatter_dimension=0, tiled=True)
    grad_docs = lax.psum(row_share, "col")
    return (hidden, grad_docs, grad_weight)


def solution(mesh):
    in_specs = (
        P(("row", "col"), None),
        P(("row", "col"), None, None, None),
        P(("row", "col"), None),
        P(("row", "col"), None),
        P(("row", "col"), None),
        P(),
        P("row", None),
        P(),
    )
    out_specs = (P(("row", "col"), None), P("row", None), P())
    return jax.shard_map(
        per_device, mesh=mesh, in_specs=in_specs, out_specs=out_specs, check_vma=False
    )
```

profile of v0, /device:TPU:0, one launch (start us, length us, event | category | flops | bytes accessed | tf_op | source)
XLA Modules:
  0.0 621.5 jit_solution(9641399624754386184)
XLA Ops:
  8.0 0.0 copy-start
  8.0 0.7 convert_bitcast_fusion.2
  8.8 0.7 copy.23
  9.5 7.1 %all-to-all-start = ((bf16[16,1,4]{2,1,0:T(2,128)(2,1)}), bf16[16,1,4]{2,1,0:T(2,128)(2,1)S(1)}, u32[]{:S(2)}, u32[]{:S(2)}) async-start(bf16[16,1,4]{2,1,0:T(2,128)(2,1)} %copy.23), calls=%async_computation | async-start | bytes 16384 | tf_op jit(solution)/shard_map/all_to_all | solution.py:23
  16.6 0.7 convert_bitcast_fusion.1
  17.3 0.7 copy.24
  18.0 0.7 compare_select_fusion
  18.7 0.1 copy.25
  18.8 0.1 reshape.51
  18.9 9.8 %gather_fusion = bf16[64,256,512]{2,1,0:T(8,128)(2,1)} fusion(bf16[16,256,512]{2,1,0:T(8,128)(2,1)} %bitcast.53, s32[1024]{0:T(1024)S(1)} %pad_clamp_fusion), kind=kCustom, calls=%fused_computation | custom fusion | bytes 33554688 | tf_op jit(solution)/shard_map/gather | solution.py:17
  28.6 0.0 all-to-all-done
  28.6 7.2 %all-to-all-start.1 = ((bf16[16,1,4]{2,1,0:T(2,128)(2,1)}), bf16[16,1,4]{2,1,0:T(2,128)(2,1)S(1)}, u32[]{:S(2)}, u32[]{:S(2)}) async-start(bf16[16,1,4]{2,1,0:T(2,128)(2,1)} %copy.24), calls=%async_computation.1 | async-start | bytes 16384 | tf_op jit(solution)/shard_map/all_to_all | solution.py:26
  35.9 19.3 %convert_bitcast_fusion = bf16[16,4,256,512]{2,3,1,0:T(8,128)(2,1)} fusion(bf16[16,4,256,512]{3,2,1,0:T(8,128)(2,1)} %bitcast.52, bf16[16,4,256,256]{3,2,1,0:T(8,128)(2,1)} %param.9), kind=kOutput, calls=%fused_computation.4 | convolution fusion | flops 4303355904 | bytes 41943040 | tf_op jit(solution)/shard_map/pqij,pqjd->pqid/dot_general | solution.py:18
  55.1 0.0 copy-start.6
  55.1 0.0 copy-start.5
  55.1 0.0 all-to-all-done.1
  55.1 7.4 %all-to-all-start.2 = ((bf16[16,4,256,512]{2,3,1,0:T(8,128)(2,1)}), bf16[16,4,256,512]{2,3,1,0:T(8,128)(2,1)}, u32[]{:S(2)}, u32[]{:S(2)}) async-start(bf16[16,4,256,512]{2,3,1,0:T(8,128)(2,1)} %convert_bitcast_fusion), calls=%async_computation.2 | async-start | bytes 33554432 | tf_op jit(solution)/shard_map/all_to_all | solution.py:22
  62.6 0.0 reduce-scatter.2.cloned.1.call-start
  62.6 0.0 copy-done.6
  62.7 0.0 copy-done.5
  62.7 14.5 %all_gather.3 = bf16[512,512]{1,0:T(8,128)(2,1)S(1)} all-gather(bf16[64,512]{1,0:T(8,128)(2,1)S(1)} %copy-done.5), channel_id=1, replica_groups=mesh['row'=8,'col'=16] {'row'}, dimensions={0}, use_global_device_ids=true | all-gather | bytes 589824 | tf_op jit(solution)/shard_map/all_gather | solution.py:48
  77.2 0.1 reshape.47
  77.3 0.1 reshape.48
  77.4 0.1 select_reduce_fusion
  77.5 229.1 %all-to-all-done.2 = bf16[16,4,256,512]{2,3,1,0:T(8,128)(2,1)} async-done(((bf16[16,4,256,512]{2,3,1,0:T(8,128)(2,1)}), bf16[16,4,256,512]{2,3,1,0:T(8,128)(2,1)}, u32[]{:S(2)}, u32[]{:S(2)}) %all-to-all-start.2) | async-done | bytes 16777248 | tf_op jit(solution)/shard_map/all_to_all | solution.py:22
  306.7 24.3 %copy.33 = bf16[8,8,256,512]{3,1,2,0:T(8,128)(2,1)} copy(bf16[8,8,256,512]{2,3,1,0:T(8,128)(2,1)} %bitcast.36) | data formatting | bytes 33554432
  331.0 9.2 %divide_convert_fusion = bf16[16,256,512]{2,0,1:T(8,128)(2,1)S(1)} fusion(bf16[16,256,512]{2,1,0:T(8,128)(2,1)} %bitcast.54, f32[16]{0:T(128)S(1)} %broadcast_add_fusion, f32[64]{0:T(128)S(1)} %reshape.48, f32[64]{0:T(128)S(1)} %reshape.47, bf16[8,8,256,512]{3,1,2,0:T(8,128)(2,1)} %copy.33), kind=kOutput, calls=%fused_computation.10 | convolution fusion | flops 278923264 | bytes 25166400 | tf_op jit(solution)/shard_map/dot_general | solution.py:36
  340.2 2.4 copy.30
  342.6 0.0 copy-start.4
  342.6 0.0 copy-done
  342.6 5.7 multiply_convert_fusion.1
  348.3 0.0 copy-done.4
  348.3 0.0 copy-start.2
  348.3 10.1 %fusion.3 = bf16[512,4096]{0,1:T(8,128)(2,1)S(1)} fusion(bf16[4096,512]{1,0:T(8,128)(2,1)S(1)} %get-tuple-element.13, bf16[512,512]{1,0:T(8,128)(2,1)S(1)} %all_gather.3, s32[512]{0:T(512)S(1)} %bitcast.63, s32[512]{0:T(512)S(1)} %bitcast.64, s32[512]{0:T(512)S(1)} %bitcast.58, s32[512]{0:T(512)S(1)} %bitcast.59, s32[512]{0:T(512)S(1)} %bitcast.60, ...), kind=kOutput, calls=%fused_computation.6 | convolution fusion | flops 2195718144 | bytes 8945664 | tf_op jit(solution)/shard_map/nd,ld->nl/dot_general | solution.py:49
  358.3 0.0 copy-done.2
  358.3 0.0 copy-start.3
  358.4 1.9 copy-done.3
  360.3 3.3 fusion.15
  363.6 0.0 reduce-scatter.2.cloned.1.call-update
  363.6 0.3 all-reduce.5.cloned.1.call-start
  363.9 0.0 copy-start.1
  363.9 12.6 %fusion.6 = f32[512,512]{1,0:T(8,128)} fusion(bf16[4096,512]{1,0:T(8,128)(2,1)} %bitcast.56, f32[4096,512]{1,0:T(8,128)} %get-tuple-element.12, bf16[512,4096]{0,1:T(8,128)(2,1)} %copy-done.3, bf16[512,512]{1,0:T(8,128)(2,1)S(1)} %all_gather.3), kind=kOutput, calls=%fused_computation.11 | convolution fusion | flops 4313841664 | bytes 18350080 | tf_op jit(solution)/shard_map/la,lb->ab/dot_general | solution.py:63
  376.5 0.0 all-reduce.5.cloned.1.call-update
  376.6 0.0 all-reduce.3.cloned.1.call-start
  376.6 21.8 %reduce-scatter.2.cloned.1.call-done = f32[64,512]{1,0:T(8,128)} async-done(((f32[512,512]{1,0:T(8,128)}), f32[64,512]{1,0:T(8,128)}) %reduce-scatter.2.cloned.1.call-update) | async-done | bytes 131088 | tf_op jit(solution)/shard_map/reduce_scatter | solution.py:65
  398.4 0.0 all-reduce.3.cloned.1.call-update
  398.5 127.3 %all-reduce.5.cloned.1.call-done = f32[512,512]{1,0:T(8,128)} async-done(((f32[512,512]{1,0:T(8,128)}), f32[512,512]{1,0:T(8,128)}) %all-reduce.5.cloned.1.call-update) | async-done | bytes 1048592 | tf_op jit(solution)/shard_map/psum | solution.py:64
  525.7 84.6 %all-reduce.3.cloned.1.call-done = f32[64,512]{1,0:T(8,128)} async-done(((f32[64,512]{1,0:T(8,128)}), f32[64,512]{1,0:T(8,128)}) %all-reduce.3.cloned.1.call-update) | async-done | bytes 131088 | tf_op jit(solution)/shard_map/psum | solution.py:66
  610.3 1.6 copy.44
  611.8 2.3 copy.45
  614.1 0.0 copy-done.1
  (6 shorter events, 0.1 us)
Async XLA Ops:
  8.0 334.6 %copy-start = (bf16[512,512]{1,0:T(8,128)(2,1)S(1)}, bf16[512,512]{1,0:T(8,128)(2,1)}, u32[]{:S(2)}) copy-start(bf16[512,512]{1,0:T(8,128)(2,1)} %param.13) | copy-start | bytes 1572868
  9.5 19.2 %all-to-all-start = ((bf16[16,1,4]{2,1,0:T(2,128)(2,1)}), bf16[16,1,4]{2,1,0:T(2,128)(2,1)S(1)}, u32[]{:S(2)}, u32[]{:S(2)}) async-start(bf16[16,1,4]{2,1,0:T(2,128)(2,1)} %copy.23), calls=%async_computation | async-start | bytes 16384 | tf_op jit(solution)/shard_map/all_to_all | solution.py:23
  28.6 26.5 %all-to-all-start.1 = ((bf16[16,1,4]{2,1,0:T(2,128)(2,1)}), bf16[16,1,4]{2,1,0:T(2,128)(2,1)S(1)}, u32[]{:S(2)}, u32[]{:S(2)}) async-start(bf16[16,1,4]{2,1,0:T(2,128)(2,1)} %copy.24), calls=%async_computation.1 | async-start | bytes 16384 | tf_op jit(solution)/shard_map/all_to_all | solution.py:26
  55.1 7.5 %copy-start.6 = (s32[512,8]{0,1:T(8,128)S(1)}, s32[512,8]{0,1:T(8,128)}, u32[]{:S(2)}) copy-start(s32[512,8]{0,1:T(8,128)} %param.15) | copy-start | bytes 49156
  55.1 7.5 %copy-start.5 = (bf16[64,512]{1,0:T(8,128)(2,1)S(1)}, bf16[64,512]{1,0:T(8,128)(2,1)}, u32[]{:S(2)}) copy-start(bf16[64,512]{1,0:T(8,128)(2,1)} %param.14) | copy-start | bytes 196612
  55.1 251.5 %all-to-all-start.2 = ((bf16[16,4,256,512]{2,3,1,0:T(8,128)(2,1)}), bf16[16,4,256,512]{2,3,1,0:T(8,128)(2,1)}, u32[]{:S(2)}, u32[]{:S(2)}) async-start(bf16[16,4,256,512]{2,3,1,0:T(8,128)(2,1)} %convert_bitcast_fusion), calls=%async_computation.2 | async-start | bytes 33554432 | tf_op jit(solution)/shard_map/all_to_all | solution.py:22
  62.6 335.9 %reduce-scatter.2.cloned.1.call-start = ((), (), s32[]{:S(2)}) async-start(), calls=%async_computation.4 | async-start | bytes 1179648 | tf_op jit(solution)/shard_map/reduce_scatter | solution.py:65
  342.6 5.7 copy-start.4
  348.3 10.1 %copy-start.2 = (bf16[4096,512]{1,0:T(8,128)(2,1)}, bf16[4096,512]{1,0:T(8,128)(2,1)S(1)}, u32[]{:S(2)}) copy-start(bf16[4096,512]{1,0:T(8,128)(2,1)S(1)} %get-tuple-element.13) | copy-start | bytes 12582916
  358.3 1.9 copy-start.3
  363.6 162.1 %all-reduce.5.cloned.1.call-start = ((), (), s32[]{:S(2)}) async-start(), calls=%async_computation.6 | async-start | bytes 2097152 | tf_op jit(solution)/shard_map/psum | solution.py:64
  363.9 250.2 %copy-start.1 = (bf16[512,512]{1,0:T(8,128)(2,1)S(1)}, bf16[512,512]{1,0:T(8,128)(2,1)}, u32[]{:S(2)}) copy-start(bf16[512,512]{1,0:T(8,128)(2,1)} %param.13) | copy-start | bytes 1572868
  376.6 233.7 %all-reduce.3.cloned.1.call-start = ((), (), s32[]{:S(2)}) async-start(), calls=%async_computation.5 | async-start | bytes 262144 | tf_op jit(solution)/shard_map/psum | solution.py:66
Sparse Core Ops, SparseCore 0:
  363.8 34.6 reduce-scatter.1
Sparse Core Ops, SparseCore 1:
  376.6 149.0 all-reduce.4
  528.8 81.4 all-reduce.2
where the time goes:
time: 623 us; the launch traced here: 622 us
  waiting for transfers between devices  463 us (74%)
  matrix products  60.1 us (10%)
  local copies, waits for them, and re-layouts  44 us (7%)
  starting transfers between devices  22.1 us (4%)
  between operations  15.7 us (3%)
  blocking collectives  14.5 us (2%)
    all_to_all x1, waiting for transfers between devices, per_device(): lax.all_to_all(messages, 'col', split_axis=0, concat_axis=0, tiled=True)  229 us
    psum x1, waiting for transfers between devices, per_device(): grad_weight = lax.psum(weight_part, ('row', 'col'))  127 us
    psum x1, waiting for transfers between devices, per_device(): grad_docs = lax.psum(row_share, 'col')  84.6 us
    unnamed x17, local copies, waits for them, and re-layouts  30.1 us
    reduce_scatter x1, waiting for transfers between devices, per_device(): lax.psum_scatter(doc_grad, 'row', scatter_dimension=0, tiled=True)  21.8 us
    dot_general x1, matrix products, per_device(): jnp.einsum('pqij,pqjd->pqid', tiles, picked, preferred_element_type=jnp.f...  19.3 us
    all_gather x1, blocking collectives, per_device(): piece = lax.all_gather(docs, 'row', axis=0, tiled=True)  14.5 us
    dot_general x1, matrix products, per_device(): jnp.einsum('la,lb->ab', agg, dpre, preferred_element_type=jnp.float32)  12.6 us
  transfers between devices with their start and end apart: 6, of which 4 were waited for; matrix products, arithmetic and copies ran while one was open for 7% of the time, Pallas kernels for 0%

commit v1 on v0

--- a/solution.py
+++ b/solution.py
@@ -2,6 +2,15 @@
 import jax.numpy as jnp
 from jax import lax
 from jax.sharding import PartitionSpec as P
+
+
+def add_in_pairs(x, axis):
+    size = lax.axis_size(axis)
+    total, stride = (x, 1)
+    while stride < size:
+        total = total + lax.ppermute(total, axis, [(i, i ^ stride) for i in range(size)])
+        stride = 2 * stride
+    return total
 
 
 def per_device(emb, tiles, msg_src, msg_dst, msg_count, weight, docs, doc_labels):
@@ -63,7 +72,7 @@
     weight_part = jnp.einsum("la,lb->ab", agg, dpre, preferred_element_type=jnp.float32)
     grad_weight = lax.psum(weight_part, ("row", "col"))
     row_share = lax.psum_scatter(doc_grad, "row", scatter_dimension=0, tiled=True)
-    grad_docs = lax.psum(row_share, "col")
+    grad_docs = add_in_pairs(row_share, "col")
     return (hidden, grad_docs, grad_weight)
 
 

time: 623 us -> 571 us (0.917)
  waiting for transfers between devices: 463 us -> 402 us
  starting transfers between devices: 22.1 us -> 30.8 us
    psum x1 -> x0, waiting for transfers between devices: 84.6 us -> none  [per_device(): grad_docs = lax.psum(row_share, 'col')]
    reduce_scatter x1, waiting for transfers between devices: 21.8 us -> 34.4 us  [per_device(): lax.psum_scatter(doc_grad, 'row', scatter_dimension=0, tiled=True)]
    ppermute x0 -> x4, waiting for transfers between devices: none -> 11.7 us  [add_in_pairs(): lax.ppermute(total, axis, [(i, i ^ stride) for i in range(size)])]
    ppermute x0 -> x4, starting transfers between devices: none -> 8.93 us  [add_in_pairs(): lax.ppermute(total, axis, [(i, i ^ stride) for i in range(size)])]
    unnamed x17 -> x18, local copies, waits for them, and re-layouts: 30.1 us -> 28.5 us
  transfers between devices with their start and end apart: 6 -> 9, of which waited for: 4 -> 6; matrix products, arithmetic and copies ran while one was open for 7% -> 8% of each run, Pallas kernels for 0% -> 0%
where the time goes in v1:
time: 571 us; the launch traced here: 568 us
  waiting for transfers between devices  402 us (70%)
  matrix products  60.1 us (11%)
  local copies, waits for them, and re-layouts  42.4 us (7%)
  starting transfers between devices  30.8 us (5%)
  between operations  15.7 us (3%)
  blocking collectives  14.5 us (3%)
    all_to_all x1, waiting for transfers between devices, per_device(): lax.all_to_all(messages, 'col', split_axis=0, concat_axis=0, tiled=True)  229 us
    psum x1, waiting for transfers between devices, per_device(): grad_weight = lax.psum(weight_part, ('row', 'col'))  127 us
    reduce_scatter x1, waiting for transfers between devices, per_device(): lax.psum_scatter(doc_grad, 'row', scatter_dimension=0, tiled=True)  34.4 us
    unnamed x18, local copies, waits for them, and re-layouts  28.5 us
    dot_general x1, matrix products, per_device(): jnp.einsum('pqij,pqjd->pqid', tiles, picked, preferred_element_type=jnp.f...  19.2 us
    all_gather x1, blocking collectives, per_device(): piece = lax.all_gather(docs, 'row', axis=0, tiled=True)  14.5 us
    dot_general x1, matrix products, per_device(): jnp.einsum('la,lb->ab', agg, dpre, preferred_element_type=jnp.float32)  12.6 us
    ppermute x4, waiting for transfers between devices, add_in_pairs(): lax.ppermute(total, axis, [(i, i ^ stride) for i in range(size)])  11.7 us
  transfers between devices with their start and end apart: 9, of which 6 were waited for; matrix products, arithmetic and copies ran while one was open for 8% of the time, Pallas kernels for 0%

profile of v1, /device:TPU:0, one launch (start us, length us, event | category | flops | bytes accessed | tf_op | source)
XLA Modules:
  0.0 568.5 jit_solution(17761258584590048342)
XLA Ops:
  8.0 0.0 copy-start
  8.0 0.7 convert_bitcast_fusion.2
  8.8 0.7 copy.23
  9.5 7.1 %all-to-all-start = ((bf16[16,1,4]{2,1,0:T(2,128)(2,1)}), bf16[16,1,4]{2,1,0:T(2,128)(2,1)S(1)}, u32[]{:S(2)}, u32[]{:S(2)}) async-start(bf16[16,1,4]{2,1,0:T(2,128)(2,1)} %copy.23), calls=%async_computation | async-start | bytes 16384 | tf_op jit(solution)/shard_map/all_to_all | solution.py:32
  16.6 0.7 convert_bitcast_fusion.1
  17.3 0.7 copy.24
  18.0 0.7 compare_select_fusion
  18.7 0.1 copy.25
  18.8 0.1 reshape.51
  18.9 9.8 %gather_fusion = bf16[64,256,512]{2,1,0:T(8,128)(2,1)} fusion(bf16[16,256,512]{2,1,0:T(8,128)(2,1)} %bitcast.53, s32[1024]{0:T(1024)S(1)} %pad_clamp_fusion), kind=kCustom, calls=%fused_computation | custom fusion | bytes 33554688 | tf_op jit(solution)/shard_map/gather | solution.py:26
  28.7 0.0 all-to-all-done
  28.7 7.2 %all-to-all-start.1 = ((bf16[16,1,4]{2,1,0:T(2,128)(2,1)}), bf16[16,1,4]{2,1,0:T(2,128)(2,1)S(1)}, u32[]{:S(2)}, u32[]{:S(2)}) async-start(bf16[16,1,4]{2,1,0:T(2,128)(2,1)} %copy.24), calls=%async_computation.1 | async-start | bytes 16384 | tf_op jit(solution)/shard_map/all_to_all | solution.py:35
  35.9 19.2 %convert_bitcast_fusion = bf16[16,4,256,512]{2,3,1,0:T(8,128)(2,1)} fusion(bf16[16,4,256,512]{3,2,1,0:T(8,128)(2,1)} %bitcast.52, bf16[16,4,256,256]{3,2,1,0:T(8,128)(2,1)} %param.9), kind=kOutput, calls=%fused_computation.4 | convolution fusion | flops 4303355904 | bytes 41943040 | tf_op jit(solution)/shard_map/pqij,pqjd->pqid/dot_general | solution.py:27
  55.1 0.0 copy-start.7
  55.1 0.0 copy-start.6
  55.1 0.0 all-to-all-done.1
  55.1 7.4 %all-to-all-start.2 = ((bf16[16,4,256,512]{2,3,1,0:T(8,128)(2,1)}), bf16[16,4,256,512]{2,3,1,0:T(8,128)(2,1)}, u32[]{:S(2)}, u32[]{:S(2)}) async-start(bf16[16,4,256,512]{2,3,1,0:T(8,128)(2,1)} %convert_bitcast_fusion), calls=%async_computation.2 | async-start | bytes 33554432 | tf_op jit(solution)/shard_map/all_to_all | solution.py:31
  62.5 0.0 reduce-scatter.2.cloned.1.call-start
  62.6 0.0 copy-done.7
  62.6 0.0 copy-done.6
  62.6 14.5 %all_gather.3 = bf16[512,512]{1,0:T(8,128)(2,1)S(1)} all-gather(bf16[64,512]{1,0:T(8,128)(2,1)S(1)} %copy-done.6), channel_id=1, replica_groups=mesh['row'=8,'col'=16] {'row'}, dimensions={0}, use_global_device_ids=true | all-gather | bytes 589824 | tf_op jit(solution)/shard_map/all_gather | solution.py:57
  77.1 0.1 reshape.47
  77.3 0.1 reshape.48
  77.4 0.1 select_reduce_fusion
  77.5 229.1 %all-to-all-done.2 = bf16[16,4,256,512]{2,3,1,0:T(8,128)(2,1)} async-done(((bf16[16,4,256,512]{2,3,1,0:T(8,128)(2,1)}), bf16[16,4,256,512]{2,3,1,0:T(8,128)(2,1)}, u32[]{:S(2)}, u32[]{:S(2)}) %all-to-all-start.2) | async-done | bytes 16777248 | tf_op jit(solution)/shard_map/all_to_all | solution.py:31
  306.6 24.3 %copy.33 = bf16[8,8,256,512]{3,1,2,0:T(8,128)(2,1)} copy(bf16[8,8,256,512]{2,3,1,0:T(8,128)(2,1)} %bitcast.36) | data formatting | bytes 33554432
  330.9 9.2 %divide_convert_fusion = bf16[16,256,512]{2,0,1:T(8,128)(2,1)S(1)} fusion(bf16[16,256,512]{2,1,0:T(8,128)(2,1)} %bitcast.54, f32[16]{0:T(128)S(1)} %broadcast_add_fusion, f32[64]{0:T(128)S(1)} %reshape.48, f32[64]{0:T(128)S(1)} %reshape.47, bf16[8,8,256,512]{3,1,2,0:T(8,128)(2,1)} %copy.33), kind=kOutput, calls=%fused_computation.10 | convolution fusion | flops 278923264 | bytes 25166400 | tf_op jit(solution)/shard_map/dot_general | solution.py:45
  340.1 2.4 copy.30
  342.5 0.0 copy-start.4
  342.5 0.0 copy-done
  342.5 5.7 multiply_convert_fusion.1
  348.2 0.0 copy-done.4
  348.2 0.0 copy-start.2
  348.2 10.1 %fusion.3 = bf16[512,4096]{0,1:T(8,128)(2,1)S(1)} fusion(bf16[4096,512]{1,0:T(8,128)(2,1)S(1)} %get-tuple-element.13, bf16[512,512]{1,0:T(8,128)(2,1)S(1)} %all_gather.3, s32[512]{0:T(512)S(1)} %bitcast.63, s32[512]{0:T(512)S(1)} %bitcast.64, s32[512]{0:T(512)S(1)} %bitcast.58, s32[512]{0:T(512)S(1)} %bitcast.59, s32[512]{0:T(512)S(1)} %bitcast.60, ...), kind=kOutput, calls=%fused_computation.6 | convolution fusion | flops 2195718144 | bytes 8945664 | tf_op jit(solution)/shard_map/nd,ld->nl/dot_general | solution.py:58
  358.3 0.0 copy-done.2
  358.3 0.0 copy-start.3
  358.3 1.9 copy-done.3
  360.2 3.3 fusion.15
  363.5 0.0 reduce-scatter.2.cloned.1.call-update
  363.5 0.0 all-reduce.2.cloned.1.call-start
  363.6 34.4 %reduce-scatter.2.cloned.1.call-done = f32[64,512]{1,0:T(8,128)} async-done(((f32[512,512]{1,0:T(8,128)}), f32[64,512]{1,0:T(8,128)}) %reduce-scatter.2.cloned.1.call-update) | async-done | bytes 131088 | tf_op jit(solution)/shard_map/reduce_scatter | solution.py:74
  398.0 1.4 collective-permute-start
  399.4 0.0 copy-start.5
  399.4 0.0 copy-start.1
  399.4 12.6 %fusion.6 = f32[512,512]{1,0:T(8,128)} fusion(bf16[4096,512]{1,0:T(8,128)(2,1)} %bitcast.56, f32[4096,512]{1,0:T(8,128)} %get-tuple-element.12, bf16[512,4096]{0,1:T(8,128)(2,1)} %copy-done.3, bf16[512,512]{1,0:T(8,128)(2,1)S(1)} %all_gather.3), kind=kOutput, calls=%fused_computation.11 | convolution fusion | flops 4313841664 | bytes 18350080 | tf_op jit(solution)/shard_map/la,lb->ab/dot_general | solution.py:72
  412.0 0.0 all-reduce.2.cloned.1.call-update
  412.1 0.0 collective-permute-done
  412.1 0.0 copy-done.5
  412.1 2.9 collective-permute-start.1
  415.0 3.7 collective-permute-done.1
  418.7 1.5 collective-permute-start.2
  420.2 4.4 collective-permute-done.2
  424.6 3.1 collective-permute-start.3
  427.8 3.6 collective-permute-done.3
  431.4 0.7 add.70
  432.1 126.7 %all-reduce.2.cloned.1.call-done = f32[512,512]{1,0:T(8,128)} async-done(((f32[512,512]{1,0:T(8,128)}), f32[512,512]{1,0:T(8,128)}) %all-reduce.2.cloned.1.call-update) | async-done | bytes 1048592 | tf_op jit(solution)/shard_map/psum | solution.py:73
  558.8 2.3 copy.43
  561.0 0.0 copy-done.1
  (9 shorter events, 0.1 us)
Async XLA Ops:
  8.0 334.5 %copy-start = (bf16[512,512]{1,0:T(8,128)(2,1)S(1)}, bf16[512,512]{1,0:T(8,128)(2,1)}, u32[]{:S(2)}) copy-start(bf16[512,512]{1,0:T(8,128)(2,1)} %param.13) | copy-start | bytes 1572868
  9.5 19.2 %all-to-all-start = ((bf16[16,1,4]{2,1,0:T(2,128)(2,1)}), bf16[16,1,4]{2,1,0:T(2,128)(2,1)S(1)}, u32[]{:S(2)}, u32[]{:S(2)}) async-start(bf16[16,1,4]{2,1,0:T(2,128)(2,1)} %copy.23), calls=%async_computation | async-start | bytes 16384 | tf_op jit(solution)/shard_map/all_to_all | solution.py:32
  28.7 26.4 %all-to-all-start.1 = ((bf16[16,1,4]{2,1,0:T(2,128)(2,1)}), bf16[16,1,4]{2,1,0:T(2,128)(2,1)S(1)}, u32[]{:S(2)}, u32[]{:S(2)}) async-start(bf16[16,1,4]{2,1,0:T(2,128)(2,1)} %copy.24), calls=%async_computation.1 | async-start | bytes 16384 | tf_op jit(solution)/shard_map/all_to_all | solution.py:35
  55.1 7.5 %copy-start.7 = (s32[512,8]{0,1:T(8,128)S(1)}, s32[512,8]{0,1:T(8,128)}, u32[]{:S(2)}) copy-start(s32[512,8]{0,1:T(8,128)} %param.15) | copy-start | bytes 49156
  55.1 7.5 %copy-start.6 = (bf16[64,512]{1,0:T(8,128)(2,1)S(1)}, bf16[64,512]{1,0:T(8,128)(2,1)}, u32[]{:S(2)}) copy-start(bf16[64,512]{1,0:T(8,128)(2,1)} %param.14) | copy-start | bytes 196612
  55.1 251.5 %all-to-all-start.2 = ((bf16[16,4,256,512]{2,3,1,0:T(8,128)(2,1)}), bf16[16,4,256,512]{2,3,1,0:T(8,128)(2,1)}, u32[]{:S(2)}, u32[]{:S(2)}) async-start(bf16[16,4,256,512]{2,3,1,0:T(8,128)(2,1)} %convert_bitcast_fusion), calls=%async_computation.2 | async-start | bytes 33554432 | tf_op jit(solution)/shard_map/all_to_all | solution.py:31
  62.5 335.5 %reduce-scatter.2.cloned.1.call-start = ((), (), s32[]{:S(2)}) async-start(), calls=%async_computation.4 | async-start | bytes 1179648 | tf_op jit(solution)/shard_map/reduce_scatter | solution.py:74
  342.5 5.7 copy-start.4
  348.2 10.1 %copy-start.2 = (bf16[4096,512]{1,0:T(8,128)(2,1)}, bf16[4096,512]{1,0:T(8,128)(2,1)S(1)}, u32[]{:S(2)}) copy-start(bf16[4096,512]{1,0:T(8,128)(2,1)S(1)} %get-tuple-element.13) | copy-start | bytes 12582916
  358.3 1.9 copy-start.3
  363.5 195.2 %all-reduce.2.cloned.1.call-start = ((), (), s32[]{:S(2)}) async-start(), calls=%async_computation.5 | async-start | bytes 2097152 | tf_op jit(solution)/shard_map/psum | solution.py:73
  398.0 14.0 %collective-permute-start = (f32[64,512]{1,0:T(8,128)}, f32[64,512]{1,0:T(8,128)S(1)}, u32[]{:S(2)}, u32[]{:S(2)}) collective-permute-start(f32[64,512]{1,0:T(8,128)} %reduce-scatter.2.cloned.1.call-done), channel_id=1, source_target_pairs={{0,1},{1,0},{2,3},{3,2},{4,5},{5,4},{6,7},{7,6},{8,9},{9,8},{10,11... | collective-permute-start | bytes 393224 | tf_op jit(solution)/shard_map/ppermute | solution.py:11
  399.4 12.7 %copy-start.5 = (f32[64,512]{1,0:T(8,128)S(1)}, f32[64,512]{1,0:T(8,128)}, u32[]{:S(2)}) copy-start(f32[64,512]{1,0:T(8,128)} %reduce-scatter.2.cloned.1.call-done) | copy-start | bytes 393220
  399.4 161.6 %copy-start.1 = (bf16[512,512]{1,0:T(8,128)(2,1)S(1)}, bf16[512,512]{1,0:T(8,128)(2,1)}, u32[]{:S(2)}) copy-start(bf16[512,512]{1,0:T(8,128)(2,1)} %param.13) | copy-start | bytes 1572868
  412.1 6.6 %collective-permute-start.1 = (f32[64,512]{1,0:T(8,128)S(1)}, f32[64,512]{1,0:T(8,128)S(1)}, u32[]{:S(2)}, u32[]{:S(2)}) collective-permute-start(f32[64,512]{1,0:T(8,128)S(1)} %add.67), channel_id=1, source_target_pairs={{0,2},{1,3},{2,0},{3,1},{4,6},{5,7},{6,4},{7,5},{8,10},{9,11},{10,... | collective-permute-start | bytes 393224 | tf_op jit(solution)/shard_map/ppermute | solution.py:11
  418.7 5.9 %collective-permute-start.2 = (f32[64,512]{1,0:T(8,128)S(1)}, f32[64,512]{1,0:T(8,128)S(1)}, u32[]{:S(2)}, u32[]{:S(2)}) collective-permute-start(f32[64,512]{1,0:T(8,128)S(1)} %add.68), channel_id=1, source_target_pairs={{0,4},{1,5},{2,6},{3,7},{4,0},{5,1},{6,2},{7,3},{8,12},{9,13},{10,... | collective-permute-start | bytes 393224 | tf_op jit(solution)/shard_map/ppermute | solution.py:11
  424.6 6.7 %collective-permute-start.3 = (f32[64,512]{1,0:T(8,128)S(1)}, f32[64,512]{1,0:T(8,128)S(1)}, u32[]{:S(2)}, u32[]{:S(2)}) collective-permute-start(f32[64,512]{1,0:T(8,128)S(1)} %add.69), channel_id=1, source_target_pairs={{0,8},{1,9},{2,10},{3,11},{4,12},{5,13},{6,14},{7,15},{8,0},{9,1},... | collective-permute-start | bytes 393224 | tf_op jit(solution)/shard_map/ppermute | solution.py:11
Sparse Core Ops, SparseCore 0:
  363.7 34.3 reduce-scatter.1
Sparse Core Ops, SparseCore 1:
  412.1 146.6 all-reduce.1
